TPU v7x, 256 devices: a whole 4x4x8 slice. The times are simulated.
256 devices in a mesh: cuts: 4 (over y), blk: 64 (over x, z, core).
Axes of the slice: x: 4, y: 4, z: 8, core: 2. Of those that a mesh axis runs over, the one named last changes fastest.
Arguments:
- gap_load: float32 [4, 128, 2, 256, 128], P('cuts', 'blk'), may hold values from -24 to 24
- offsets: int32 [4, 128, 2], P('cuts', 'blk'), may hold values from -1 to 255, as said below
- corner_map: int32 [4, 128, 4], P('cuts', 'blk'), may hold values from -1 to 511, as said below
- flexibility: float32 [4, 128, 1024, 1024], P('cuts', 'blk'), may hold values from -0.5 to 4.5, as said below
- coupling: float32 [4, 128, 12, 1024], P('cuts', 'blk'), may hold values from -1.25 to 1.25
- corner_rows: float32 [4, 128, 12, 1536], P('cuts', 'blk'), may hold values from -0.1 to 1.1, as said below
Outputs:
- multipliers: float32 [4, 128, 2, 256, 128], P('cuts', 'blk')
- residual: float32 [4, 128, 2, 256, 128], P('cuts', 'blk')
Inputs may be any that keep to these rules, and one draw needn't show every extreme that they name: `offsets`: on an interface owned by a subdomain, the neighbour's dof k matches the owner's dof (k + offset) mod 256; -1 marks an interface without multipliers: the tunnel's far end, or one that touches an excavated subdomain. `corner_map`: entries k = 0, 1, 2, 3 are the corners at near-left, near-right, far-left, far-right. Entry 2 of subdomain (r, c) is never -1, and every node is entry 2 of exactly one subdomain; the same node is entry 3 of (r, (c - 1) mod 128) and, for r + 1 < 4, entries 0 of (r + 1, c) and 1 of (r + 1, (c - 1) mod 128), and no other entry. -1 marks a clamped corner at the tunnel's near end. `flexibility`: each block is symmetric positive definite. `corner_rows`: row 3 k + j of a subdomain is row 3 m + j of one symmetric positive definite matrix of order 3 * 512, with m = corner_map entry k; zero rows where that entry is -1.
All inputs are finite; a program needn't handle non-finite values.
Results may differ from a plain program's by a relative error of at most 0.00021.
Values sent between devices are 32-bit elements; how exact they have to be, the bound alone decides.
A program may use at most 64 MiB of HBM per device.

v0:
```python
import jax
import jax.numpy as jnp
from jax import lax
from jax.sharding import PartitionSpec as P

ITERS = 3
HIGH = lax.Precision.HIGHEST


def from_behind(value, axis, steps):
    count = lax.axis_size(axis)
    first, last = (max(0, -steps), min(count, count - steps))
    return lax.ppermute(value, axis, [(source, source + steps) for source in range(first, last)])


def passed_along(value, axis, steps):
    count = lax.axis_size(axis)
    pairs = [(source, (source + steps) % count) for source in range(count)]
    return lax.ppermute(value, axis, pairs)


def rotate(values, amounts, orient):
    face_size = values.shape[-2]
    indices = (jnp.arange(face_size, dtype=jnp.int32) + orient * amounts[..., None]) % face_size
    return jnp.take_along_axis(values, indices[..., None], axis=-2)


def corner_indices(corner_map, dof_count):
    spread = 3 * corner_map[..., None] + jnp.arange(3, dtype=jnp.int32)
    spread = jnp.where(corner_map[..., None] >= 0, spread, dof_count)
    return spread.reshape(corner_map.shape[0], corner_map.shape[1], 12)


def inner_sum(first, second):
    return jnp.sum(first * second, axis=(0, 1, 2, 3))


def squares(residual):
    return lax.psum(inner_sum(residual, residual), ("cuts", "blk"))


def per_device(gap_load, offsets, corner_map, flexibility, coupling, corner_rows):
    cycle_count, circ_count, _, face_size, load_count = gap_load.shape
    dof_count = corner_rows.shape[-1]
    active = (offsets >= 0).astype(jnp.float32)[..., None, None]
    corner_dofs = corner_indices(corner_map, dof_count)
    residual = gap_load * active
    multipliers = jnp.zeros_like(residual)
    direction = residual
    norm_now = squares(residual)
    for iteration in range(ITERS):
        sent_far = -rotate(direction[:, :, 0], offsets[:, :, 0], 1)
        sent_right = -rotate(direction[:, :, 1], offsets[:, :, 1], 1)
        edge_near = from_behind(sent_far[-1], "cuts", 1)
        edge_left = passed_along(sent_right[:, -1], "blk", 1)
        nearside = jnp.concatenate([edge_near[None], sent_far[:-1]], axis=0)
        leftside = jnp.concatenate([edge_left[:, None], sent_right[:, :-1]], axis=1)
        loads = jnp.stack([nearside, direction[:, :, 0], leftside, direction[:, :, 1]], axis=2)
        loads = loads.reshape(cycle_count, circ_count, 4 * face_size, load_count)
        operator_corner_terms = jnp.einsum("rcki,rcin->rckn", coupling, loads, precision=HIGH)
        partial_value = jnp.zeros((dof_count, load_count), jnp.float32)
        partial_value = partial_value.at[corner_dofs.reshape(-1)].add(
            operator_corner_terms.reshape(-1, load_count), mode="drop"
        )
        coarse = lax.psum(partial_value, ("cuts", "blk"))
        corner_values = jnp.einsum("rckm,mn->rckn", corner_rows, coarse, precision=HIGH)
        moved = jnp.einsum("rcij,rcjn->rcin", flexibility, loads, precision=HIGH)
        moved = moved + jnp.einsum("rcki,rckn->rcin", coupling, corner_values, precision=HIGH)
        moved = moved.reshape(cycle_count, circ_count, 4, face_size, load_count)
        from_far = from_behind(moved[0, :, 0], "cuts", -1)
        from_right = passed_along(moved[:, 0, 2], "blk", -1)
        far_near = jnp.concatenate([moved[1:, :, 0], from_far[None]], axis=0)
        right_left = jnp.concatenate([moved[:, 1:, 2], from_right[:, None]], axis=1)
        jump_far = moved[:, :, 1] - rotate(far_near, offsets[:, :, 0], -1)
        jump_right = moved[:, :, 3] - rotate(right_left, offsets[:, :, 1], -1)
        mapped = jnp.stack([jump_far, jump_right], axis=2) * active
        step_size = norm_now / lax.psum(inner_sum(direction, mapped), ("cuts", "blk"))
        multipliers = multipliers + step_size * direction
        residual = residual - step_size * mapped
        norm_next = squares(residual)
        direction = residual + norm_next / norm_now * direction
        norm_now = norm_next
    return (multipliers, residual)


def solution(mesh):
    in_specs = (
        P("cuts", "blk", None, None, None),
        P("cuts", "blk", None),
        P("cuts", "blk", None),
        P("cuts", "blk", None, None),
        P("cuts", "blk", None, None),
        P("cuts", "blk", None, None),
    )
    out_specs = (P("cuts", "blk", None, None, None), P("cuts", "blk", None, None, None))
    return jax.shard_map(
        per_device, mesh=mesh, in_specs=in_specs, out_specs=out_specs, check_vma=False
    )
```

profile of v0, /device:TPU:1, one launch (start us, length us, event | category | flops | bytes accessed | tf_op | source)
XLA Modules:
  0.0 1306.6 jit_solution(7525697432891195552)
XLA Ops:
  10.4 3.7 gather_fusion.1
  14.3 3.1 collective-permute-start.1
  17.6 3.7 gather_fusion
  21.4 3.2 collective-permute-start
  25.0 4.6 collective-permute-done
  33.4 11.0 fusion.4
  44.4 248.0 %all-reduce.5.cloned.1.call-done = f32[1536,128]{1,0:T(8,128)} async-done(((f32[1536,128]{1,0:T(8,128)}), f32[1536,128]{1,0:T(8,128)}) %all-reduce.5.cloned.1.call-update) | async-done | bytes 786448 | tf_op jit(solution)/shard_map/psum | solution.py:65
  298.3 2.4 collective-permute-start.3
  303.1 3.7 gather_fusion.3
  308.9 3.7 gather_fusion.2
  312.9 78.9 %all-reduce = (f32[128]{0:T(128)S(1)}, f32[128]{0:T(128)S(1)}) all-reduce(f32[128]{0:T(128)S(1)} %get-tuple-element.8, f32[128]{0:T(128)S(1)} %get-tuple-element.7), channel_id=1, replica_groups=mesh['cuts'=4,'blk'=64] {'cuts','blk'}, use_global_device_ids=true, to_apply=%region_1.2 | all-reduce | flops 256 | bytes 2048 | tf_op jit(solution)/shard_map/psum | solution.py:39
  392.0 72.6 %psum.66 = f32[128]{0:T(128)S(1)} all-reduce(f32[128]{0:T(128)S(1)} %multiply_reduce_fusion.3), channel_id=1, replica_groups=mesh['cuts'=4,'blk'=64] {'cuts','blk'}, use_global_device_ids=true, to_apply=%region_7.9 | all-reduce | flops 128 | bytes 1024 | tf_op jit(solution)/shard_map/psum | solution.py:39
  464.9 3.7 gather_fusion.4
  468.7 3.7 gather_fusion.5
  472.5 2.4 collective-permute-start.4
  475.0 2.7 collective-permute-start.5
  483.9 11.0 fusion.2
  494.9 243.5 %all-reduce.7.cloned.1.call-done = f32[1536,128]{1,0:T(8,128)} async-done(((f32[1536,128]{1,0:T(8,128)}), f32[1536,128]{1,0:T(8,128)}) %all-reduce.7.cloned.1.call-update) | async-done | bytes 786448 | tf_op jit(solution)/shard_map/psum | solution.py:65
  750.5 3.7 gather_fusion.7
  755.2 3.7 gather_fusion.6
  759.9 80.2 %psum.68 = f32[128]{0:T(128)S(1)} all-reduce(f32[128]{0:T(128)S(1)} %multiply_reduce_fusion.2), channel_id=1, replica_groups=mesh['cuts'=4,'blk'=64] {'cuts','blk'}, use_global_device_ids=true, to_apply=%region_11.13 | all-reduce | flops 128 | bytes 1024 | tf_op jit(solution)/shard_map/psum | solution.py:77
  840.9 72.8 %psum.69 = f32[128]{0:T(128)S(1)} all-reduce(f32[128]{0:T(128)S(1)} %get-tuple-element.15), channel_id=1, replica_groups=mesh['cuts'=4,'blk'=64] {'cuts','blk'}, use_global_device_ids=true, to_apply=%region_13.15 | all-reduce | flops 128 | bytes 1024 | tf_op jit(solution)/shard_map/psum | solution.py:39
  915.3 3.7 gather_fusion.8
  919.8 3.7 gather_fusion.9
  925.8 2.7 collective-permute-start.9
  936.7 12.0 fusion
  948.8 242.0 %all-reduce.9.cloned.1.call-done = f32[1536,128]{1,0:T(8,128)} async-done(((f32[1536,128]{1,0:T(8,128)}), f32[1536,128]{1,0:T(8,128)}) %all-reduce.9.cloned.1.call-update) | async-done | bytes 786448 | tf_op jit(solution)/shard_map/psum | solution.py:65
  1192.5 3.3 fusion.6
  1200.1 2.3 collective-permute-start.11
  1210.8 3.7 gather_fusion.11
  1215.9 3.7 gather_fusion.10
  1220.0 77.9 %psum.71 = f32[128]{0:T(128)S(1)} all-reduce(f32[128]{0:T(128)S(1)} %multiply_reduce_fusion), channel_id=1, replica_groups=mesh['cuts'=4,'blk'=64] {'cuts','blk'}, use_global_device_ids=true, to_apply=%region_17.19 | all-reduce | flops 128 | bytes 1024 | tf_op jit(solution)/shard_map/psum | solution.py:77
  (161 shorter events, 71.3 us)
Async XLA Ops:
  7.2 285.2 %copy-start = (f32[1,2,12,1536]{3,1,2,0:T(2,128)S(1)}, f32[1,2,12,1536]{3,1,2,0:T(2,128)}, u32[]{:S(2)}) copy-start(f32[1,2,12,1536]{3,1,2,0:T(2,128)} %param.13) | copy-start | bytes 442372
  7.2 17.4 %copy-start.12 = (s32[1,2,4]{2,1,0:T(2,128)S(1)}, s32[1,2,4]{2,1,0:T(2,128)}, u32[]{:S(2)}) copy-start(s32[1,2,4]{2,1,0:T(2,128)} %param.10) | copy-start | bytes 100
  7.2 23.5 %copy-start.2 = (f32[1,2,12,1024]{3,1,2,0:T(2,128)S(1)}, f32[1,2,12,1024]{3,1,2,0:T(2,128)}, u32[]{:S(2)}) copy-start(f32[1,2,12,1024]{3,1,2,0:T(2,128)} %param.12) | copy-start | bytes 294916
  7.2 285.2 %all-reduce.5.cloned.1.call-start = ((), (), s32[]{:S(2)}) async-start(), calls=%async_computation | async-start | bytes 1572864 | tf_op jit(solution)/shard_map/psum | solution.py:65
  9.0 463.4 %copy-start.5 = (pred[2,256]{1,0:T(4,128)(4,1)}, pred[2,256]{1,0:T(4,128)(4,1)S(1)}, u32[]{:S(2)}) copy-start(pred[2,256]{1,0:T(4,128)(4,1)S(1)} %and_bitcast_fusion.2) | copy-start | bytes 1540
  14.3 10.7 collective-permute-start.1
  17.5 451.1 %copy-start.7 = (pred[2,256]{1,0:T(4,128)(4,1)}, pred[2,256]{1,0:T(4,128)(4,1)S(1)}, u32[]{:S(2)}) copy-start(pred[2,256]{1,0:T(4,128)(4,1)S(1)} %and_bitcast_fusion.3) | copy-start | bytes 1540
  21.4 8.3 collective-permute-start
  25.0 457.0 %copy-start.13 = (s32[24]{0:T(128)}, s32[24]{0:T(128)S(1)}, u32[]{:S(2)}) copy-start(s32[24]{0:T(128)S(1)} %fusion.45) | copy-start | bytes 292
  33.3 705.1 %all-reduce.7.cloned.1.call-start = ((), (), s32[]{:S(2)}) async-start(), calls=%async_computation.1 | async-start | bytes 1572864 | tf_op jit(solution)/shard_map/psum | solution.py:65
  292.4 20.3 %copy-start.1 = (f32[1,2,2,256,128]{4,3,2,1,0:T(8,128)S(1)}, f32[1,2,2,256,128]{4,3,2,1,0:T(8,128)}, u32[]{:S(2)}) copy-start(f32[1,2,2,256,128]{4,3,2,1,0:T(8,128)} %param.8) | copy-start | bytes 1572868
  298.3 4.8 collective-permute-start.3
  301.8 7.1 collective-permute-start.2
  464.6 16.3 %copy-start.14 = (f32[128]{0:T(128)}, f32[128]{0:T(128)S(1)}, u32[]{:S(2)}) copy-start(f32[128]{0:T(128)S(1)} %psum.66) | copy-start | bytes 1540
  464.6 16.3 %copy-start.8 = (f32[128]{0:T(128)}, f32[128]{0:T(128)S(1)}, u32[]{:S(2)}) copy-start(f32[128]{0:T(128)S(1)} %div.16) | copy-start | bytes 1540
  472.5 7.4 collective-permute-start.4
  475.0 4.6 collective-permute-start.5
  483.6 707.2 %all-reduce.9.cloned.1.call-start = ((), (), s32[]{:S(2)}) async-start(), calls=%async_computation.2 | async-start | bytes 1572864 | tf_op jit(solution)/shard_map/psum | solution.py:65
  744.9 4.7 collective-permute-start.7
  748.1 7.1 collective-permute-start.6
  755.2 168.2 %copy-start.6 = (pred[2,256]{1,0:T(4,128)(4,1)S(1)}, pred[2,256]{1,0:T(4,128)(4,1)}, u32[]{:S(2)}) copy-start(pred[2,256]{1,0:T(4,128)(4,1)} %copy-done.5) | copy-start | bytes 1540
  840.7 91.5 %copy-start.10 = (f32[128]{0:T(128)}, f32[128]{0:T(128)S(1)}, u32[]{:S(2)}) copy-start(f32[128]{0:T(128)S(1)} %div.17) | copy-start | bytes 1540
  840.9 73.4 %copy-start.3 = (f32[1,2,2,256,128]{4,3,1,2,0:T(8,128)}, f32[1,2,2,256,128]{4,3,1,2,0:T(8,128)S(1)}, u32[]{:S(2)}) copy-start(f32[1,2,2,256,128]{4,3,1,2,0:T(8,128)S(1)} %get-tuple-element.16) | copy-start | bytes 1572868
  913.7 20.2 %copy-start.15 = (f32[128]{0:T(128)}, f32[128]{0:T(128)S(1)}, u32[]{:S(2)}) copy-start(f32[128]{0:T(128)S(1)} %psum.69) | copy-start | bytes 1540
  923.6 7.2 collective-permute-start.8
  925.8 4.6 collective-permute-start.9
  1192.5 105.4 %copy-start.4 = (f32[1,2,2,256,128]{4,3,1,2,0:T(8,128)S(1)}, f32[1,2,2,256,128]{4,3,1,2,0:T(8,128)}, u32[]{:S(2)}) copy-start(f32[1,2,2,256,128]{4,3,1,2,0:T(8,128)} %copy-done.3) | copy-start | bytes 1572868
  1192.5 105.4 %copy-start.9 = (f32[128]{0:T(128)S(1)}, f32[128]{0:T(128)}, u32[]{:S(2)}) copy-start(f32[128]{0:T(128)} %copy-done.8) | copy-start | bytes 1540
  1192.5 105.4 %copy-start.11 = (f32[128]{0:T(128)S(1)}, f32[128]{0:T(128)}, u32[]{:S(2)}) copy-start(f32[128]{0:T(128)} %copy-done.10) | copy-start | bytes 1540
  1195.8 102.1 %copy-start.16 = (f32[128]{0:T(128)S(1)}, f32[128]{0:T(128)}, u32[]{:S(2)}) copy-start(f32[128]{0:T(128)} %copy-done.15) | copy-start | bytes 1540
  1200.1 9.8 collective-permute-start.11
  1208.6 7.3 collective-permute-start.10
Sparse Core Ops, SparseCore 0:
  33.4 258.9 all-reduce.4
  483.7 254.6 all-reduce.6
  936.8 253.8 all-reduce.8
where the time goes:
time: 1320 us; the launch traced here: 1310 us
  waiting for transfers between devices  746 us (57%)
  blocking collectives  382 us (29%)
  local copies, waits for them, and re-layouts  68.4 us (5%)
  matrix products  49.6 us (4%)
  starting transfers between devices  27.4 us (2%)
  other arithmetic  18.2 us (1%)
  between operations  14.7 us (1%)
    psum x3, waiting for transfers between devices, per_device(): coarse = lax.psum(partial_value, ('cuts', 'blk'))  733 us
    psum x3, blocking collectives, squares(): return lax.psum(inner_sum(residual, residual), ('cuts', 'blk'))  224 us
    psum x2, blocking collectives, per_device(): lax.psum(inner_sum(direction, mapped), ('cuts', 'blk'))  158 us
    gather x12, local copies, waits for them, and re-layouts, rotate(): return jnp.take_along_axis(values, indices[..., None], axis=-2)  43.9 us
    dot_general x3, matrix products, per_device(): moved = jnp.einsum('rcij,rcjn->rcin', flexibility, loads, precision=HIGH)  34.1 us
  transfers between devices with their start and end apart: 15, of which 12 were waited for; matrix products, arithmetic and copies ran while one was open for 5% of the time, Pallas kernels for 0%

commit v1 on v0

--- a/solution.py
+++ b/solution.py
@@ -62,7 +62,7 @@
         partial_value = partial_value.at[corner_dofs.reshape(-1)].add(
             operator_corner_terms.reshape(-1, load_count), mode="drop"
         )
-        coarse = lax.psum(partial_value, ("cuts", "blk"))
+        coarse = lax.psum(lax.psum(partial_value, "cuts"), "blk")
         corner_values = jnp.einsum("rckm,mn->rckn", corner_rows, coarse, precision=HIGH)
         moved = jnp.einsum("rcij,rcjn->rcin", flexibility, loads, precision=HIGH)
         moved = moved + jnp.einsum("rcki,rckn->rcin", coupling, corner_values, precision=HIGH)

time: 1320 us -> 1260 us (0.955)
  waiting for transfers between devices: 746 us -> 691 us
    psum x3 -> x6, waiting for transfers between devices: 733 us -> 678 us  [per_device(): coarse = lax.psum(lax.psum(partial_value, 'cuts'), 'blk')]
  transfers between devices with their start and end apart: 15 -> 18, of which waited for: 12 -> 15; matrix products, arithmetic and copies ran while one was open for 5% -> 5% of each run, Pallas kernels for 0% -> 0%
where the time goes in v1:
time: 1260 us; the launch traced here: 1250 us
  waiting for transfers between devices  691 us (55%)
  blocking collectives  382 us (30%)
  local copies, waits for them, and re-layouts  68.4 us (5%)
  matrix products  49.6 us (4%)
  starting transfers between devices  27.6 us (2%)
  other arithmetic  18 us (1%)
  between operations  15.1 us (1%)
    psum x6, waiting for transfers between devices, per_device(): coarse = lax.psum(lax.psum(partial_value, 'cuts'), 'blk')  678 us
    psum x3, blocking collectives, squares(): return lax.psum(inner_sum(residual, residual), ('cuts', 'blk'))  224 us
    psum x2, blocking collectives, per_device(): lax.psum(inner_sum(direction, mapped), ('cuts', 'blk'))  158 us
    gather x12, local copies, waits for them, and re-layouts, rotate(): return jnp.take_along_axis(values, indices[..., None], axis=-2)  43.9 us
    dot_general x3, matrix products, per_device(): moved = jnp.einsum('rcij,rcjn->rcin', flexibility, loads, precision=HIGH)  34.1 us
  transfers between devices with their start and end apart: 18, of which 15 were waited for; matrix products, arithmetic and copies ran while one was open for 5% of the time, Pallas kernels for 0%

profile of v1, /device:TPU:1, one launch (start us, length us, event | category | flops | bytes accessed | tf_op | source)
XLA Modules:
  0.0 1252.1 jit_solution(6547937003601236646)
XLA Ops:
  10.4 3.7 gather_fusion.1
  14.3 3.1 collective-permute-start.1
  17.6 3.7 gather_fusion
  21.4 3.2 collective-permute-start
  24.8 4.8 collective-permute-done
  33.6 51.0 %all-reduce.8.cloned.1.call-done = f32[1536,128]{1,0:T(8,128)} async-done(((f32[1536,128]{1,0:T(8,128)}), f32[1536,128]{1,0:T(8,128)}) %all-reduce.8.cloned.1.call-update) | async-done | bytes 786448 | tf_op jit(solution)/shard_map/psum | solution.py:65
  84.6 11.0 fusion.4
  95.7 179.0 %all-reduce.10.cloned.1.call-done = f32[1536,128]{1,0:T(8,128)} async-done(((f32[1536,128]{1,0:T(8,128)}), f32[1536,128]{1,0:T(8,128)}) %all-reduce.10.cloned.1.call-update) | async-done | bytes 786448 | tf_op jit(solution)/shard_map/psum | solution.py:65
  285.5 3.7 gather_fusion.3
  291.2 3.7 gather_fusion.2
  295.3 78.9 %all-reduce = (f32[128]{0:T(128)S(1)}, f32[128]{0:T(128)S(1)}) all-reduce(f32[128]{0:T(128)S(1)} %get-tuple-element.8, f32[128]{0:T(128)S(1)} %get-tuple-element.7), channel_id=1, replica_groups=mesh['cuts'=4,'blk'=64] {'cuts','blk'}, use_global_device_ids=true, to_apply=%region_1.2 | all-reduce | flops 256 | bytes 2048 | tf_op jit(solution)/shard_map/psum | solution.py:39
  374.4 72.4 %psum.88 = f32[128]{0:T(128)S(1)} all-reduce(f32[128]{0:T(128)S(1)} %multiply_reduce_fusion.3), channel_id=1, replica_groups=mesh['cuts'=4,'blk'=64] {'cuts','blk'}, use_global_device_ids=true, to_apply=%region_8.10 | all-reduce | flops 128 | bytes 1024 | tf_op jit(solution)/shard_map/psum | solution.py:39
  447.1 3.7 gather_fusion.4
  450.9 3.7 gather_fusion.5
  457.0 2.7 collective-permute-start.5
  465.6 46.1 %all-reduce.12.cloned.1.call-done = f32[1536,128]{1,0:T(8,128)} async-done(((f32[1536,128]{1,0:T(8,128)}), f32[1536,128]{1,0:T(8,128)}) %all-reduce.12.cloned.1.call-update) | async-done | bytes 786448 | tf_op jit(solution)/shard_map/psum | solution.py:65
  512.0 11.0 fusion.2
  523.0 178.7 %all-reduce.14.cloned.1.call-done = f32[1536,128]{1,0:T(8,128)} async-done(((f32[1536,128]{1,0:T(8,128)}), f32[1536,128]{1,0:T(8,128)}) %all-reduce.14.cloned.1.call-update) | async-done | bytes 786448 | tf_op jit(solution)/shard_map/psum | solution.py:65
  713.8 3.7 gather_fusion.7
  718.6 3.7 gather_fusion.6
  723.2 80.2 %psum.91 = f32[128]{0:T(128)S(1)} all-reduce(f32[128]{0:T(128)S(1)} %multiply_reduce_fusion.2), channel_id=1, replica_groups=mesh['cuts'=4,'blk'=64] {'cuts','blk'}, use_global_device_ids=true, to_apply=%region_13.15 | all-reduce | flops 128 | bytes 1024 | tf_op jit(solution)/shard_map/psum | solution.py:77
  804.3 72.8 %psum.92 = f32[128]{0:T(128)S(1)} all-reduce(f32[128]{0:T(128)S(1)} %get-tuple-element.15), channel_id=1, replica_groups=mesh['cuts'=4,'blk'=64] {'cuts','blk'}, use_global_device_ids=true, to_apply=%region_15.17 | all-reduce | flops 128 | bytes 1024 | tf_op jit(solution)/shard_map/psum | solution.py:39
  878.6 3.7 gather_fusion.8
  883.1 3.7 gather_fusion.9
  889.2 2.7 collective-permute-start.9
  900.0 46.0 %all-reduce.16.cloned.1.call-done = f32[1536,128]{1,0:T(8,128)} async-done(((f32[1536,128]{1,0:T(8,128)}), f32[1536,128]{1,0:T(8,128)}) %all-reduce.16.cloned.1.call-update) | async-done | bytes 786448 | tf_op jit(solution)/shard_map/psum | solution.py:65
  946.1 12.0 fusion
  958.1 177.7 %all-reduce.18.cloned.1.call-done = f32[1536,128]{1,0:T(8,128)} async-done(((f32[1536,128]{1,0:T(8,128)}), f32[1536,128]{1,0:T(8,128)}) %all-reduce.18.cloned.1.call-update) | async-done | bytes 786448 | tf_op jit(solution)/shard_map/psum | solution.py:65
  1137.5 3.3 fusion.6
  1156.0 3.7 gather_fusion.11
  1161.1 3.7 gather_fusion.10
  1165.1 77.9 %psum.95 = f32[128]{0:T(128)S(1)} all-reduce(f32[128]{0:T(128)S(1)} %multiply_reduce_fusion), channel_id=1, replica_groups=mesh['cuts'=4,'blk'=64] {'cuts','blk'}, use_global_device_ids=true, to_apply=%region_20.22 | all-reduce | flops 128 | bytes 1024 | tf_op jit(solution)/shard_map/psum | solution.py:77
  (170 shorter events, 78.6 us)
Async XLA Ops:
  7.2 267.5 %copy-start = (f32[1,2,12,1536]{3,1,2,0:T(2,128)S(1)}, f32[1,2,12,1536]{3,1,2,0:T(2,128)}, u32[]{:S(2)}) copy-start(f32[1,2,12,1536]{3,1,2,0:T(2,128)} %param.13) | copy-start | bytes 442372
  7.2 23.5 %copy-start.2 = (f32[1,2,12,1024]{3,1,2,0:T(2,128)S(1)}, f32[1,2,12,1024]{3,1,2,0:T(2,128)}, u32[]{:S(2)}) copy-start(f32[1,2,12,1024]{3,1,2,0:T(2,128)} %param.12) | copy-start | bytes 294916
  7.2 77.4 %all-reduce.8.cloned.1.call-start = ((), (), s32[]{:S(2)}) async-start(), calls=%async_computation | async-start | bytes 1572864 | tf_op jit(solution)/shard_map/psum | solution.py:65
  9.0 445.5 %copy-start.5 = (pred[2,256]{1,0:T(4,128)(4,1)}, pred[2,256]{1,0:T(4,128)(4,1)S(1)}, u32[]{:S(2)}) copy-start(pred[2,256]{1,0:T(4,128)(4,1)S(1)} %and_bitcast_fusion.2) | copy-start | bytes 1540
  14.3 10.5 collective-permute-start.1
  17.5 433.3 %copy-start.7 = (pred[2,256]{1,0:T(4,128)(4,1)}, pred[2,256]{1,0:T(4,128)(4,1)S(1)}, u32[]{:S(2)}) copy-start(pred[2,256]{1,0:T(4,128)(4,1)S(1)} %and_bitcast_fusion.3) | copy-start | bytes 1540
  21.4 8.3 collective-permute-start
  24.8 439.2 %copy-start.13 = (s32[24]{0:T(128)}, s32[24]{0:T(128)S(1)}, u32[]{:S(2)}) copy-start(s32[24]{0:T(128)S(1)} %fusion.45) | copy-start | bytes 292
  33.3 241.4 %all-reduce.10.cloned.1.call-start = ((), (), s32[]{:S(2)}) async-start(), calls=%async_computation.1 | async-start | bytes 1572864 | tf_op jit(solution)/shard_map/psum | solution.py:65
  84.6 427.1 %all-reduce.12.cloned.1.call-start = ((), (), s32[]{:S(2)}) async-start(), calls=%async_computation.2 | async-start | bytes 1572864 | tf_op jit(solution)/shard_map/psum | solution.py:65
  274.7 20.4 %copy-start.1 = (f32[1,2,2,256,128]{4,3,2,1,0:T(8,128)S(1)}, f32[1,2,2,256,128]{4,3,2,1,0:T(8,128)}, u32[]{:S(2)}) copy-start(f32[1,2,2,256,128]{4,3,2,1,0:T(8,128)} %param.8) | copy-start | bytes 1572868
  280.5 4.9 collective-permute-start.3
  284.1 7.1 collective-permute-start.2
  454.7 7.2 collective-permute-start.4
  457.0 4.6 collective-permute-start.5
  465.6 236.1 %all-reduce.14.cloned.1.call-start = ((), (), s32[]{:S(2)}) async-start(), calls=%async_computation.3 | async-start | bytes 1572864 | tf_op jit(solution)/shard_map/psum | solution.py:65
  511.7 434.4 %all-reduce.16.cloned.1.call-start = ((), (), s32[]{:S(2)}) async-start(), calls=%async_computation.4 | async-start | bytes 1572864 | tf_op jit(solution)/shard_map/psum | solution.py:65
  708.1 4.7 collective-permute-start.7
  711.5 7.1 collective-permute-start.6
  718.6 168.2 %copy-start.6 = (pred[2,256]{1,0:T(4,128)(4,1)S(1)}, pred[2,256]{1,0:T(4,128)(4,1)}, u32[]{:S(2)}) copy-start(pred[2,256]{1,0:T(4,128)(4,1)} %copy-done.5) | copy-start | bytes 1540
  804.0 91.4 %copy-start.10 = (f32[128]{0:T(128)}, f32[128]{0:T(128)S(1)}, u32[]{:S(2)}) copy-start(f32[128]{0:T(128)S(1)} %div.17) | copy-start | bytes 1540
  804.3 73.4 %copy-start.3 = (f32[1,2,2,256,128]{4,3,1,2,0:T(8,128)}, f32[1,2,2,256,128]{4,3,1,2,0:T(8,128)S(1)}, u32[]{:S(2)}) copy-start(f32[1,2,2,256,128]{4,3,1,2,0:T(8,128)S(1)} %get-tuple-element.16) | copy-start | bytes 1572868
  877.1 20.2 %copy-start.15 = (f32[128]{0:T(128)}, f32[128]{0:T(128)S(1)}, u32[]{:S(2)}) copy-start(f32[128]{0:T(128)S(1)} %psum.92) | copy-start | bytes 1540
  886.9 7.2 collective-permute-start.8
  889.2 4.6 collective-permute-start.9
  900.0 235.8 %all-reduce.18.cloned.1.call-start = ((), (), s32[]{:S(2)}) async-start(), calls=%async_computation.5 | async-start | bytes 1572864 | tf_op jit(solution)/shard_map/psum | solution.py:65
  1137.5 105.6 %copy-start.4 = (f32[1,2,2,256,128]{4,3,1,2,0:T(8,128)S(1)}, f32[1,2,2,256,128]{4,3,1,2,0:T(8,128)}, u32[]{:S(2)}) copy-start(f32[1,2,2,256,128]{4,3,1,2,0:T(8,128)} %copy-done.3) | copy-start | bytes 1572868
  1137.5 105.6 %copy-start.9 = (f32[128]{0:T(128)S(1)}, f32[128]{0:T(128)}, u32[]{:S(2)}) copy-start(f32[128]{0:T(128)} %copy-done.8) | copy-start | bytes 1540
  1137.5 105.6 %copy-start.11 = (f32[128]{0:T(128)S(1)}, f32[128]{0:T(128)}, u32[]{:S(2)}) copy-start(f32[128]{0:T(128)} %copy-done.10) | copy-start | bytes 1540
  1140.8 102.2 %copy-start.16 = (f32[128]{0:T(128)S(1)}, f32[128]{0:T(128)}, u32[]{:S(2)}) copy-start(f32[128]{0:T(128)} %copy-done.15) | copy-start | bytes 1540
  1145.1 9.9 collective-permute-start.11
  1153.8 7.3 collective-permute-start.10
  (3 other events, 49.6 us)
Sparse Core Ops, SparseCore 0:
  33.4 51.0 all-reduce.7
  88.0 186.6 all-reduce.9
  465.7 45.9 all-reduce.11
  515.0 186.6 all-reduce.13
  900.1 45.9 all-reduce.15
  949.4 186.4 all-reduce.17
